TPU v7x, 32 devices: a whole 2x2x4 slice. The times are simulated.
32 devices in a mesh: agent: 8 (over y, x, core), res: 4 (over z).
Axes of the slice: x: 2, y: 2, z: 4, core: 2. Of those that a mesh axis runs over, the one named last changes fastest.
Arguments:
- linear_cost: float32 [2048, 2048], P('agent', 'res'), may hold values from -6 to 6
- agent_type: int32 [2048], P('agent'), may hold values from 0 to 3, as said below
- block_mask: int32 [2048, 16], P('agent', 'res'), may hold values 0 or 1
- inverses: bfloat16 [4, 2048, 2048], P(None, 'res'), as said below
- cost_weight: float32 [2048], P('res'), may hold values from 0.5 to 8
- target: float32 [2048], P('res'), may hold values from -6 to 6
Outputs:
- usage: float32 [2048, 2048], P('agent', 'res')
- shared: float32 [2048], P('res')
- prices: float32 [2048], P('res')
- primal_norm: float32 [5], replicated
- dual_norm: float32 [5], replicated
Inputs may be any that keep to these rules, and one draw needn't show every extreme that they name: Each inverses[k] is exactly symmetric: inverses[k, i, j] equals inverses[k, j, i]. `agent_type`: each aligned block of 256 agents (the agents held by one device along the agent axis) holds exactly 64 agents of each type, in no particular order.
All inputs are finite; a program needn't handle non-finite values. No bound on the sum of `block_mask` on one device may be relied on, other than what follows from the above.
Results may differ from a plain program's by a relative error of at most 0.0039.
Values may be sent and summed in bfloat16 or wider, within the bound.
No kernel may reach another device: no remote copies, remote signals or barrier semaphores. Data moves between devices by JAX's collectives and lax.ppermute only.
A program may use at most 64 MiB of HBM per device.

v0:
```python
import jax
import jax.numpy as jnp
from jax import lax
from jax.sharding import PartitionSpec as P

BLK = 128
ITERS = 5
penalty = 1.0
eps = 1e-06


def on_device(linear_cost, agent_type, block_mask, inverses, cost_weight, target):
    local_agents, local_width = linear_cost.shape
    type_count = inverses.shape[0]
    group_rows = local_agents // type_count
    count = local_agents * lax.axis_size("agent")
    block_count = block_mask.shape[1]
    order = jnp.argsort(agent_type, stable=True)
    restore = jnp.argsort(order, stable=True)
    expand = jnp.broadcast_to(
        block_mask.astype(jnp.float32)[:, :, None], (local_agents, block_count, BLK)
    ).reshape(local_agents, local_width)
    usage = jnp.zeros(linear_cost.shape, jnp.float32)
    mean_usage = jnp.zeros((local_width,), jnp.float32)
    shared = jnp.zeros((local_width,), jnp.float32)
    prices = jnp.zeros((local_width,), jnp.float32)
    primal_list = []
    dual_list = []
    for iteration in range(ITERS):
        rhs = (penalty * (usage - mean_usage + shared - prices) - linear_cost).astype(jnp.bfloat16)
        grouped = rhs[order].reshape(type_count, group_rows, local_width)
        product = jnp.einsum(
            "tas,tws->taw",
            lax.all_gather(grouped, "res", axis=2, tiled=True),
            inverses,
            preferred_element_type=jnp.float32,
        )
        new_usage = product.reshape(local_agents, local_width)[restore]
        new_usage = new_usage * expand
        change_local = penalty * penalty * jnp.sum((new_usage - usage) ** 2)
        usage = new_usage
        column_sum = jnp.sum(usage, axis=0)
        usage_sum = lax.psum(column_sum, "agent")
        dual2 = lax.psum(change_local, ("agent", "res"))
        mean_usage = usage_sum / count
        shared = (cost_weight * target + penalty * (prices + mean_usage)) / (cost_weight + penalty)
        prices = prices + mean_usage - shared
        primal2 = lax.psum(count * jnp.sum((mean_usage - shared) ** 2), "res")
        primal_list.append(jnp.sqrt(primal2 + eps))
        dual_list.append(jnp.sqrt(dual2 + eps))
    primal_norm = jnp.stack(primal_list)
    dual_norm = jnp.stack(dual_list)
    return (usage, shared, prices, primal_norm, dual_norm)


def solution(mesh):
    placed = (
        P("agent", "res"),
        P("agent"),
        P("agent", "res"),
        P(None, "res", None),
        P("res"),
        P("res"),
    )
    return jax.shard_map(
        on_device,
        mesh=mesh,
        in_specs=placed,
        out_specs=(P("agent", "res"), P("res"), P("res"), P(), P()),
        check_vma=False,
    )
```

profile of v0, /device:TPU:12, one launch (start us, length us, event | category | flops | bytes accessed | tf_op | source)
XLA Modules:
  0.0 334.9 jit_solution(6932095263842248031)
XLA Ops:
  7.2 3.8 %sort.31 = (s32[256]{0:T(256)}, s32[256]{0:T(256)S(1)}) sort(s32[256]{0:T(256)} %param.7, s32[256]{0:T(256)S(1)} %iota.7), dimensions={0}, to_apply=%region_0.0 | sort | flops 2048 | bytes 4096 | tf_op jit(solution)/shard_map/jit(argsort)/sort | solution.py:18
  14.1 3.2 sort.32
  18.2 25.1 %all-gather.6.cloned.1.call-done = bf16[4,64,2048]{2,1,0:T(8,128)(2,1)} async-done(((bf16[4,64,512]{2,1,0:T(8,128)(2,1)}), bf16[4,64,2048]{2,1,0:T(8,128)(2,1)}) %all-gather.6.cloned.1.call-update) | async-done | bytes 1048592 | tf_op jit(solution)/shard_map/all_gather | solution.py:34
  43.3 6.4 %fusion.13 = f32[4,64,512]{2,1,0:T(8,128)S(1)} fusion(bf16[4,64,2048]{2,1,0:T(8,128)(2,1)} %all-gather.6.cloned.1.call-done, bf16[4,512,2048]{2,1,0:T(8,128)(2,1)} %param.9), kind=kOutput, calls=%fused_computation.56 | convolution fusion | flops 536870912 | bytes 9961472 | tf_op jit(solution)/shard_map/tas,tws->taw/dot_general | solution.py:32
  51.1 11.9 %psum.105 = f32[512]{0:T(512)S(1)} all-reduce(f32[512]{0:T(512)S(1)} %get-tuple-element.44), channel_id=1, replica_groups=mesh['agent'=8,'res'=4] {'agent'}, use_global_device_ids=true, to_apply=%region_3.4 | all-reduce | flops 512 | bytes 4096 | tf_op jit(solution)/shard_map/psum | solution.py:43
  63.7 1.9 gather_fusion.2
  65.7 27.5 %all-gather.8.cloned.1.call-done = bf16[4,64,2048]{2,1,0:T(8,128)(2,1)} async-done(((bf16[4,64,512]{2,1,0:T(8,128)(2,1)}), bf16[4,64,2048]{2,1,0:T(8,128)(2,1)}) %all-gather.8.cloned.1.call-update) | async-done | bytes 1048592 | tf_op jit(solution)/shard_map/all_gather | solution.py:34
  93.1 6.4 %fusion.14 = f32[4,64,512]{2,1,0:T(8,128)S(1)} fusion(bf16[4,64,2048]{2,1,0:T(8,128)(2,1)} %all-gather.8.cloned.1.call-done, bf16[4,512,2048]{2,1,0:T(8,128)(2,1)} %param.9), kind=kOutput, calls=%fused_computation.57 | convolution fusion | flops 536870912 | bytes 9961472 | tf_op jit(solution)/shard_map/tas,tws->taw/dot_general | solution.py:32
  100.6 11.9 %psum.106 = f32[512]{0:T(512)S(1)} all-reduce(f32[512]{0:T(512)S(1)} %get-tuple-element.42), channel_id=1, replica_groups=mesh['agent'=8,'res'=4] {'agent'}, use_global_device_ids=true, to_apply=%region_5.6 | all-reduce | flops 512 | bytes 4096 | tf_op jit(solution)/shard_map/psum | solution.py:43
  113.2 1.9 gather_fusion.4
  115.1 27.5 %all-gather.10.cloned.1.call-done = bf16[4,64,2048]{2,1,0:T(8,128)(2,1)} async-done(((bf16[4,64,512]{2,1,0:T(8,128)(2,1)}), bf16[4,64,2048]{2,1,0:T(8,128)(2,1)}) %all-gather.10.cloned.1.call-update) | async-done | bytes 1048592 | tf_op jit(solution)/shard_map/all_gather | solution.py:34
  142.6 6.4 %fusion.15 = f32[4,64,512]{2,1,0:T(8,128)S(1)} fusion(bf16[4,64,2048]{2,1,0:T(8,128)(2,1)} %all-gather.10.cloned.1.call-done, bf16[4,512,2048]{2,1,0:T(8,128)(2,1)} %param.9), kind=kOutput, calls=%fused_computation.58 | convolution fusion | flops 536870912 | bytes 9961472 | tf_op jit(solution)/shard_map/tas,tws->taw/dot_general | solution.py:32
  150.0 12.1 %psum.107 = f32[512]{0:T(512)S(1)} all-reduce(f32[512]{0:T(512)S(1)} %get-tuple-element.40), channel_id=1, replica_groups=mesh['agent'=8,'res'=4] {'agent'}, use_global_device_ids=true, to_apply=%region_7.8 | all-reduce | flops 512 | bytes 4096 | tf_op jit(solution)/shard_map/psum | solution.py:43
  162.8 1.9 gather_fusion.6
  164.8 27.4 %all-gather.12.cloned.1.call-done = bf16[4,64,2048]{2,1,0:T(8,128)(2,1)} async-done(((bf16[4,64,512]{2,1,0:T(8,128)(2,1)}), bf16[4,64,2048]{2,1,0:T(8,128)(2,1)}) %all-gather.12.cloned.1.call-update) | async-done | bytes 1048592 | tf_op jit(solution)/shard_map/all_gather | solution.py:34
  192.2 6.4 %fusion.16 = f32[4,64,512]{2,1,0:T(8,128)S(1)} fusion(bf16[4,64,2048]{2,1,0:T(8,128)(2,1)} %all-gather.12.cloned.1.call-done, bf16[4,512,2048]{2,1,0:T(8,128)(2,1)} %param.9), kind=kOutput, calls=%fused_computation.59 | convolution fusion | flops 536870912 | bytes 9961472 | tf_op jit(solution)/shard_map/tas,tws->taw/dot_general | solution.py:32
  201.5 11.9 %psum.108 = f32[512]{0:T(512)S(1)} all-reduce(f32[512]{0:T(512)S(1)} %get-tuple-element.38), channel_id=1, replica_groups=mesh['agent'=8,'res'=4] {'agent'}, use_global_device_ids=true, to_apply=%region_9.10 | all-reduce | flops 512 | bytes 4096 | tf_op jit(solution)/shard_map/psum | solution.py:43
  214.1 1.9 gather_fusion.8
  218.6 24.9 %all-gather.14.cloned.1.call-done = bf16[4,64,2048]{2,1,0:T(8,128)(2,1)} async-done(((bf16[4,64,512]{2,1,0:T(8,128)(2,1)}), bf16[4,64,2048]{2,1,0:T(8,128)(2,1)}) %all-gather.14.cloned.1.call-update) | async-done | bytes 1048592 | tf_op jit(solution)/shard_map/all_gather | solution.py:34
  243.5 6.4 %fusion.17 = f32[4,64,512]{2,1,0:T(8,128)S(1)} fusion(bf16[4,64,2048]{2,1,0:T(8,128)(2,1)} %all-gather.14.cloned.1.call-done, bf16[4,512,2048]{2,1,0:T(8,128)(2,1)} %param.9), kind=kOutput, calls=%fused_computation.60 | convolution fusion | flops 536870912 | bytes 9961472 | tf_op jit(solution)/shard_map/tas,tws->taw/dot_general | solution.py:32
  251.7 2.8 multiply_reduce_fusion
  254.5 11.9 %psum.109 = f32[512]{0:T(512)S(1)} all-reduce(f32[512]{0:T(512)S(1)} %get-tuple-element.14), channel_id=1, replica_groups=mesh['agent'=8,'res'=4] {'agent'}, use_global_device_ids=true, to_apply=%region_11.12 | all-reduce | flops 512 | bytes 4096 | tf_op jit(solution)/shard_map/psum | solution.py:43
  268.2 9.8 %all-reduce.1 = (f32[]{:T(128)}, f32[]{:T(128)}, f32[]{:T(128)}, f32[]{:T(128)}, f32[]{:T(128)}) all-reduce(f32[]{:T(128)S(6)} %mul.99, f32[]{:T(128)S(6)} %mul.100, f32[]{:T(128)S(6)} %mul.101, f32[]{:T(128)S(6)} %mul.102, f32[]{:T(128)S(6)} %mul.103), channel_id=1, replica_groups=mesh['agent'=8,'res'=4] {'res'}, use_global_device_ids=true, to_apply=%region_13.14 | all-reduce | flops 5 | bytes 40 | tf_op jit(solution)/shard_map/psum | solution.py:48
  281.3 42.5 %all-reduce = (f32[]{:T(128)}, f32[]{:T(128)}, f32[]{:T(128)}, f32[]{:T(128)}, f32[]{:T(128)}) all-reduce(f32[]{:T(128)} %get-tuple-element.13, f32[]{:T(128)} %get-tuple-element.12, f32[]{:T(128)} %get-tuple-element.11, f32[]{:T(128)} %get-tuple-element.10, f32[]{:T(128)} %get-tuple-element.9), channel_id=1, replica_groups=mesh['agent'=8,'res'=4] {'agent','res'}, use_global_device_ids=true, to_apply=%region_23.24 | all-reduce | flops 5 | bytes 40 | tf_op jit(solution)/shard_map/psum | solution.py:44
  (53 shorter events, 17.7 us)
Async XLA Ops:
  7.2 36.1 %all-gather.6.cloned.1.call-start = ((), (), s32[]{:S(2)}) async-start(), calls=%async_computation | async-start | bytes 1310720 | tf_op jit(solution)/shard_map/all_gather | solution.py:34
  14.0 79.1 %all-gather.8.cloned.1.call-start = ((), (), s32[]{:S(2)}) async-start(), calls=%async_computation.1 | async-start | bytes 1310720 | tf_op jit(solution)/shard_map/all_gather | solution.py:34
  18.1 44.9 %copy-start.1 = (f32[512]{0:T(512)S(1)}, f32[512]{0:T(512)}, u32[]{:S(2)}) copy-start(f32[512]{0:T(512)} %param.10) | copy-start | bytes 6148
  18.1 44.9 %copy-start.3 = (f32[512]{0:T(512)S(1)}, f32[512]{0:T(512)}, u32[]{:S(2)}) copy-start(f32[512]{0:T(512)} %param.11) | copy-start | bytes 6148
  18.1 45.5 %copy-start = (f32[256,512]{1,0:T(8,128)S(1)}, f32[256,512]{1,0:T(8,128)}, u32[]{:S(2)}) copy-start(f32[256,512]{1,0:T(8,128)} %param.6) | copy-start | bytes 1572868
  65.6 77.0 %all-gather.10.cloned.1.call-start = ((), (), s32[]{:S(2)}) async-start(), calls=%async_computation.2 | async-start | bytes 1310720 | tf_op jit(solution)/shard_map/all_gather | solution.py:34
  115.1 77.2 %all-gather.12.cloned.1.call-start = ((), (), s32[]{:S(2)}) async-start(), calls=%async_computation.3 | async-start | bytes 1310720 | tf_op jit(solution)/shard_map/all_gather | solution.py:34
  164.7 78.8 %all-gather.14.cloned.1.call-start = ((), (), s32[]{:S(2)}) async-start(), calls=%async_computation.4 | async-start | bytes 1310720 | tf_op jit(solution)/shard_map/all_gather | solution.py:34
  267.0 61.4 %copy-start.2 = (f32[512]{0:T(512)}, f32[512]{0:T(512)S(1)}, u32[]{:S(2)}) copy-start(f32[512]{0:T(512)S(1)} %get-tuple-element.26) | copy-start | bytes 6148
Sparse Core Ops, SparseCore 0:
  14.2 29.0 all-gather.5
  65.7 27.3 all-gather.7
  115.2 27.3 all-gather.9
  164.8 27.3 all-gather.11
  216.1 27.3 all-gather.13
where the time goes:
time: 336 us; the launch traced here: 335 us
  waiting for transfers between devices  132 us (39%)
  blocking collectives  112 us (33%)
  matrix products  31.9 us (9%)
  between operations  23.8 us (7%)
  local copies, waits for them, and re-layouts  17.4 us (5%)
  other arithmetic  17.3 us (5%)
    all_gather x5, waiting for transfers between devices, on_device(): lax.all_gather(grouped, 'res', axis=2, tiled=True)  132 us
    psum x5, blocking collectives, on_device(): usage_sum = lax.psum(column_sum, 'agent')  59.6 us
    psum x1, blocking collectives, on_device(): dual2 = lax.psum(change_local, ('agent', 'res'))  42.5 us
    dot_general x5, matrix products, on_device(): jnp.einsum('tas,tws->taw', lax.all_gather(grouped, 'res', axis=2, tiled=T...  31.9 us
    psum x1, blocking collectives, on_device(): primal2 = lax.psum(count * jnp.sum((mean_usage - shared) ** 2), 'res')  9.78 us
    gather x5, local copies, waits for them, and re-layouts, on_device(): grouped = rhs[order].reshape(type_count, group_rows, local_width)  9.27 us
  transfers between devices with their start and end apart: 5, of which 5 were waited for; matrix products, arithmetic and copies ran while one was open for 1% of the time, Pallas kernels for 0%

commit v1 on v0

--- a/solution.py
+++ b/solution.py
@@ -40,7 +40,11 @@
         change_local = penalty * penalty * jnp.sum((new_usage - usage) ** 2)
         usage = new_usage
         column_sum = jnp.sum(usage, axis=0)
-        usage_sum = lax.psum(column_sum, "agent")
+        usage_sum = column_sum
+        for hop in (1, 2, 4):
+            usage_sum = usage_sum + lax.ppermute(
+                usage_sum, "agent", [(dev, dev ^ hop) for dev in range(8)]
+            )
         dual2 = lax.psum(change_local, ("agent", "res"))
         mean_usage = usage_sum / count
         shared = (cost_weight * target + penalty * (prices + mean_usage)) / (cost_weight + penalty)

time: 336 us -> 318 us (0.946)
  blocking collectives: 112 us -> 51 us
  waiting for transfers between devices: 132 us -> 163 us
  starting transfers between devices: 0.21 us -> 10.7 us
    psum x5 -> x0, blocking collectives: 59.6 us -> none  [on_device(): usage_sum = lax.psum(column_sum, 'agent')]
    ppermute x0 -> x15, waiting for transfers between devices: none -> 28.5 us  [on_device(): lax.ppermute(usage_sum, 'agent', [(dev, dev ^ hop) for dev in range(8)])]
    ppermute x0 -> x15, starting transfers between devices: none -> 10.4 us  [on_device(): lax.ppermute(usage_sum, 'agent', [(dev, dev ^ hop) for dev in range(8)])]
  transfers between devices with their start and end apart: 5 -> 20, of which waited for: 5 -> 19; matrix products, arithmetic and copies ran while one was open for 1% -> 1% of each run, Pallas kernels for 0% -> 0%
where the time goes in v1:
time: 318 us; the launch traced here: 316 us
  waiting for transfers between devices  163 us (51%)
  blocking collectives  51 us (16%)
  matrix products  31.9 us (10%)
  between operations  24.1 us (8%)
  local copies, waits for them, and re-layouts  17.4 us (5%)
  other arithmetic  17.3 us (5%)
  starting transfers between devices  10.7 us (3%)
    all_gather x5, waiting for transfers between devices, on_device(): lax.all_gather(grouped, 'res', axis=2, tiled=True)  135 us
    psum x1, blocking collectives, on_device(): dual2 = lax.psum(change_local, ('agent', 'res'))  40.7 us
    dot_general x5, matrix products, on_device(): jnp.einsum('tas,tws->taw', lax.all_gather(grouped, 'res', axis=2, tiled=T...  31.9 us
    ppermute x15, waiting for transfers between devices, on_device(): lax.ppermute(usage_sum, 'agent', [(dev, dev ^ hop) for dev in range(8)])  28.5 us
    ppermute x15, starting transfers between devices, on_device(): lax.ppermute(usage_sum, 'agent', [(dev, dev ^ hop) for dev in range(8)])  10.4 us
    psum x1, blocking collectives, on_device(): primal2 = lax.psum(count * jnp.sum((mean_usage - shared) ** 2), 'res')  10.3 us
    gather x5, local copies, waits for them, and re-layouts, on_device(): grouped = rhs[order].reshape(type_count, group_rows, local_width)  9.29 us
    gather x5, local copies, waits for them, and re-layouts, on_device(): new_usage = product.reshape(local_agents, local_width)[restore]  6.45 us
  transfers between devices with their start and end apart: 20, of which 19 were waited for; matrix products, arithmetic and copies ran while one was open for 1% of the time, Pallas kernels for 0%

profile of v1, /device:TPU:12, one launch (start us, length us, event | category | flops | bytes accessed | tf_op | source)
XLA Modules:
  0.0 315.9 jit_solution(9412975653726188234)
XLA Ops:
  7.2 3.8 %sort.31 = (s32[256]{0:T(256)}, s32[256]{0:T(256)S(1)}) sort(s32[256]{0:T(256)} %param.7, s32[256]{0:T(256)S(1)} %iota.7), dimensions={0}, to_apply=%region_0.0 | sort | flops 2048 | bytes 4096 | tf_op jit(solution)/shard_map/jit(argsort)/sort | solution.py:18
  14.1 3.2 %sort.32 = (s32[256]{0:T(256)}, s32[256]{0:T(256)S(1)}) sort(s32[256]{0:T(256)S(1)} %get-tuple-element.7, s32[256]{0:T(256)S(1)} %iota.8), dimensions={0}, to_apply=%region_1.2 | sort | flops 2048 | bytes 4096 | tf_op jit(solution)/shard_map/jit(argsort)/sort | solution.py:19
  18.2 25.1 %all-gather.6.cloned.1.call-done = bf16[4,64,2048]{2,1,0:T(8,128)(2,1)} async-done(((bf16[4,64,512]{2,1,0:T(8,128)(2,1)}), bf16[4,64,2048]{2,1,0:T(8,128)(2,1)}) %all-gather.6.cloned.1.call-update) | async-done | bytes 1048592 | tf_op jit(solution)/shard_map/all_gather | solution.py:34
  43.3 6.4 %fusion.6 = f32[4,64,512]{2,1,0:T(8,128)S(1)} fusion(bf16[4,64,2048]{2,1,0:T(8,128)(2,1)} %all-gather.6.cloned.1.call-done, bf16[4,512,2048]{2,1,0:T(8,128)(2,1)} %param.9), kind=kOutput, calls=%fused_computation.50 | convolution fusion | flops 536870912 | bytes 9961472 | tf_op jit(solution)/shard_map/tas,tws->taw/dot_general | solution.py:32
  53.8 2.1 collective-permute-done.1
  56.5 3.0 collective-permute-done.2
  62.2 27.5 %all-gather.8.cloned.1.call-done = bf16[4,64,2048]{2,1,0:T(8,128)(2,1)} async-done(((bf16[4,64,512]{2,1,0:T(8,128)(2,1)}), bf16[4,64,2048]{2,1,0:T(8,128)(2,1)}) %all-gather.8.cloned.1.call-update) | async-done | bytes 1048592 | tf_op jit(solution)/shard_map/all_gather | solution.py:34
  89.6 6.4 %fusion.7 = f32[4,64,512]{2,1,0:T(8,128)S(1)} fusion(bf16[4,64,2048]{2,1,0:T(8,128)(2,1)} %all-gather.8.cloned.1.call-done, bf16[4,512,2048]{2,1,0:T(8,128)(2,1)} %param.9), kind=kOutput, calls=%fused_computation.51 | convolution fusion | flops 536870912 | bytes 9961472 | tf_op jit(solution)/shard_map/tas,tws->taw/dot_general | solution.py:32
  99.8 2.1 collective-permute-done.4
  102.5 3.0 collective-permute-done.5
  108.4 27.3 %all-gather.10.cloned.1.call-done = bf16[4,64,2048]{2,1,0:T(8,128)(2,1)} async-done(((bf16[4,64,512]{2,1,0:T(8,128)(2,1)}), bf16[4,64,2048]{2,1,0:T(8,128)(2,1)}) %all-gather.10.cloned.1.call-update) | async-done | bytes 1048592 | tf_op jit(solution)/shard_map/all_gather | solution.py:34
  135.6 6.4 %fusion.8 = f32[4,64,512]{2,1,0:T(8,128)S(1)} fusion(bf16[4,64,2048]{2,1,0:T(8,128)(2,1)} %all-gather.10.cloned.1.call-done, bf16[4,512,2048]{2,1,0:T(8,128)(2,1)} %param.9), kind=kOutput, calls=%fused_computation.52 | convolution fusion | flops 536870912 | bytes 9961472 | tf_op jit(solution)/shard_map/tas,tws->taw/dot_general | solution.py:32
  145.8 2.1 collective-permute-done.7
  148.5 3.0 collective-permute-done.8
  154.2 27.5 %all-gather.12.cloned.1.call-done = bf16[4,64,2048]{2,1,0:T(8,128)(2,1)} async-done(((bf16[4,64,512]{2,1,0:T(8,128)(2,1)}), bf16[4,64,2048]{2,1,0:T(8,128)(2,1)}) %all-gather.12.cloned.1.call-update) | async-done | bytes 1048592 | tf_op jit(solution)/shard_map/all_gather | solution.py:34
  181.6 6.4 %fusion.9 = f32[4,64,512]{2,1,0:T(8,128)S(1)} fusion(bf16[4,64,2048]{2,1,0:T(8,128)(2,1)} %all-gather.12.cloned.1.call-done, bf16[4,512,2048]{2,1,0:T(8,128)(2,1)} %param.9), kind=kOutput, calls=%fused_computation.53 | convolution fusion | flops 536870912 | bytes 9961472 | tf_op jit(solution)/shard_map/tas,tws->taw/dot_general | solution.py:32
  193.6 2.1 collective-permute-done.10
  196.3 3.0 collective-permute-done.11
  202.0 27.5 %all-gather.14.cloned.1.call-done = bf16[4,64,2048]{2,1,0:T(8,128)(2,1)} async-done(((bf16[4,64,512]{2,1,0:T(8,128)(2,1)}), bf16[4,64,2048]{2,1,0:T(8,128)(2,1)}) %all-gather.14.cloned.1.call-update) | async-done | bytes 1048592 | tf_op jit(solution)/shard_map/all_gather | solution.py:34
  229.5 6.4 %fusion.10 = f32[4,64,512]{2,1,0:T(8,128)S(1)} fusion(bf16[4,64,2048]{2,1,0:T(8,128)(2,1)} %all-gather.14.cloned.1.call-done, bf16[4,512,2048]{2,1,0:T(8,128)(2,1)} %param.9), kind=kOutput, calls=%fused_computation.54 | convolution fusion | flops 536870912 | bytes 9961472 | tf_op jit(solution)/shard_map/tas,tws->taw/dot_general | solution.py:32
  237.6 2.8 multiply_reduce_fusion
  243.1 2.1 collective-permute-done.13
  248.4 40.7 %all-reduce = (f32[]{:T(128)}, f32[]{:T(128)}, f32[]{:T(128)}, f32[]{:T(128)}, f32[]{:T(128)}) all-reduce(f32[]{:T(128)} %get-tuple-element.13, f32[]{:T(128)} %get-tuple-element.12, f32[]{:T(128)} %get-tuple-element.11, f32[]{:T(128)} %get-tuple-element.10, f32[]{:T(128)} %get-tuple-element.9), channel_id=1, replica_groups=mesh['agent'=8,'res'=4] {'agent','res'}, use_global_device_ids=true, to_apply=%region_18.19 | all-reduce | flops 5 | bytes 40 | tf_op jit(solution)/shard_map/psum | solution.py:48
  294.5 10.3 %all-reduce.1 = (f32[]{:T(128)}, f32[]{:T(128)}, f32[]{:T(128)}, f32[]{:T(128)}, f32[]{:T(128)}) all-reduce(f32[]{:T(128)S(6)} %mul.99, f32[]{:T(128)S(6)} %mul.100, f32[]{:T(128)S(6)} %mul.101, f32[]{:T(128)S(6)} %mul.102, f32[]{:T(128)S(6)} %mul.103), channel_id=1, replica_groups=mesh['agent'=8,'res'=4] {'res'}, use_global_device_ids=true, to_apply=%region_8.9 | all-reduce | flops 5 | bytes 40 | tf_op jit(solution)/shard_map/psum | solution.py:52
  (92 shorter events, 41.5 us)
Async XLA Ops:
  7.2 36.1 %all-gather.6.cloned.1.call-start = ((), (), s32[]{:S(2)}) async-start(), calls=%async_computation | async-start | bytes 1310720 | tf_op jit(solution)/shard_map/all_gather | solution.py:34
  14.0 75.6 %all-gather.8.cloned.1.call-start = ((), (), s32[]{:S(2)}) async-start(), calls=%async_computation.1 | async-start | bytes 1310720 | tf_op jit(solution)/shard_map/all_gather | solution.py:34
  18.1 41.4 %copy-start.3 = (f32[512]{0:T(512)S(1)}, f32[512]{0:T(512)}, u32[]{:S(2)}) copy-start(f32[512]{0:T(512)} %param.10) | copy-start | bytes 6148
  18.1 41.4 %copy-start.5 = (f32[512]{0:T(512)S(1)}, f32[512]{0:T(512)}, u32[]{:S(2)}) copy-start(f32[512]{0:T(512)} %param.11) | copy-start | bytes 6148
  18.1 42.0 %copy-start = (f32[256,512]{1,0:T(8,128)S(1)}, f32[256,512]{1,0:T(8,128)}, u32[]{:S(2)}) copy-start(f32[256,512]{1,0:T(8,128)} %param.6) | copy-start | bytes 1572868
  51.1 1.2 collective-permute-start
  52.3 3.6 %collective-permute-start.1 = (f32[512]{0:T(512)S(1)}, f32[512]{0:T(512)S(1)}, u32[]{:S(2)}, u32[]{:S(2)}) collective-permute-start(f32[512]{0:T(512)S(1)} %add.181), channel_id=1, source_target_pairs={{0,8},{4,12},{8,0},{12,4},{16,24},{20,28},{24,16},{28,20},{1,9},{5... | collective-permute-start | bytes 6152 | tf_op jit(solution)/shard_map/ppermute | solution.py:45
  55.9 3.6 %collective-permute-start.2 = (f32[512]{0:T(512)S(1)}, f32[512]{0:T(512)S(1)}, u32[]{:S(2)}, u32[]{:S(2)}) collective-permute-start(f32[512]{0:T(512)S(1)} %add.182), channel_id=1, source_target_pairs={{0,16},{4,20},{8,24},{12,28},{16,0},{20,4},{24,8},{28,12},{1,17},{... | collective-permute-start | bytes 6152 | tf_op jit(solution)/shard_map/ppermute | solution.py:45
  62.1 73.5 %all-gather.10.cloned.1.call-start = ((), (), s32[]{:S(2)}) async-start(), calls=%async_computation.2 | async-start | bytes 1310720 | tf_op jit(solution)/shard_map/all_gather | solution.py:34
  97.1 1.2 collective-permute-start.3
  98.3 3.6 %collective-permute-start.4 = (f32[512]{0:T(512)S(1)}, f32[512]{0:T(512)S(1)}, u32[]{:S(2)}, u32[]{:S(2)}) collective-permute-start(f32[512]{0:T(512)S(1)} %add.188), channel_id=1, source_target_pairs={{0,8},{4,12},{8,0},{12,4},{16,24},{20,28},{24,16},{28,20},{1,9},{5... | collective-permute-start | bytes 6152 | tf_op jit(solution)/shard_map/ppermute | solution.py:45
  101.9 3.6 %collective-permute-start.5 = (f32[512]{0:T(512)S(1)}, f32[512]{0:T(512)S(1)}, u32[]{:S(2)}, u32[]{:S(2)}) collective-permute-start(f32[512]{0:T(512)S(1)} %add.189), channel_id=1, source_target_pairs={{0,16},{4,20},{8,24},{12,28},{16,0},{20,4},{24,8},{28,12},{1,17},{... | collective-permute-start | bytes 6152 | tf_op jit(solution)/shard_map/ppermute | solution.py:45
  108.1 73.5 %all-gather.12.cloned.1.call-start = ((), (), s32[]{:S(2)}) async-start(), calls=%async_computation.3 | async-start | bytes 1310720 | tf_op jit(solution)/shard_map/all_gather | solution.py:34
  143.1 1.2 collective-permute-start.6
  144.3 3.6 %collective-permute-start.7 = (f32[512]{0:T(512)S(1)}, f32[512]{0:T(512)S(1)}, u32[]{:S(2)}, u32[]{:S(2)}) collective-permute-start(f32[512]{0:T(512)S(1)} %add.195), channel_id=1, source_target_pairs={{0,8},{4,12},{8,0},{12,4},{16,24},{20,28},{24,16},{28,20},{1,9},{5... | collective-permute-start | bytes 6152 | tf_op jit(solution)/shard_map/ppermute | solution.py:45
  147.9 3.6 %collective-permute-start.8 = (f32[512]{0:T(512)S(1)}, f32[512]{0:T(512)S(1)}, u32[]{:S(2)}, u32[]{:S(2)}) collective-permute-start(f32[512]{0:T(512)S(1)} %add.196), channel_id=1, source_target_pairs={{0,16},{4,20},{8,24},{12,28},{16,0},{20,4},{24,8},{28,12},{1,17},{... | collective-permute-start | bytes 6152 | tf_op jit(solution)/shard_map/ppermute | solution.py:45
  154.1 75.4 %all-gather.14.cloned.1.call-start = ((), (), s32[]{:S(2)}) async-start(), calls=%async_computation.4 | async-start | bytes 1310720 | tf_op jit(solution)/shard_map/all_gather | solution.py:34
  190.9 1.2 collective-permute-start.9
  192.2 3.6 %collective-permute-start.10 = (f32[512]{0:T(512)S(1)}, f32[512]{0:T(512)S(1)}, u32[]{:S(2)}, u32[]{:S(2)}) collective-permute-start(f32[512]{0:T(512)S(1)} %add.202), channel_id=1, source_target_pairs={{0,8},{4,12},{8,0},{12,4},{16,24},{20,28},{24,16},{28,20},{1,9},{5... | collective-permute-start | bytes 6152 | tf_op jit(solution)/shard_map/ppermute | solution.py:45
  195.8 3.6 %collective-permute-start.11 = (f32[512]{0:T(512)S(1)}, f32[512]{0:T(512)S(1)}, u32[]{:S(2)}, u32[]{:S(2)}) collective-permute-start(f32[512]{0:T(512)S(1)} %add.203), channel_id=1, source_target_pairs={{0,16},{4,20},{8,24},{12,28},{16,0},{20,4},{24,8},{28,12},{1,17},{... | collective-permute-start | bytes 6152 | tf_op jit(solution)/shard_map/ppermute | solution.py:45
  200.1 37.6 %copy-start.2 = (f32[256,512]{1,0:T(8,128)S(1)}, f32[256,512]{1,0:T(8,128)}, u32[]{:S(2)}) copy-start(f32[256,512]{1,0:T(8,128)} %copy-done.1) | copy-start | bytes 1572868
  240.5 1.2 collective-permute-start.12
  241.6 3.6 %collective-permute-start.13 = (f32[512]{0:T(512)S(1)}, f32[512]{0:T(512)S(1)}, u32[]{:S(2)}, u32[]{:S(2)}) collective-permute-start(f32[512]{0:T(512)S(1)} %add.209), channel_id=1, source_target_pairs={{0,8},{4,12},{8,0},{12,4},{16,24},{20,28},{24,16},{28,20},{1,9},{5... | collective-permute-start | bytes 6152 | tf_op jit(solution)/shard_map/ppermute | solution.py:45
  245.2 47.4 %collective-permute-start.14 = (f32[512]{0:T(512)S(1)}, f32[512]{0:T(512)S(1)}, u32[]{:S(2)}, u32[]{:S(2)}) collective-permute-start(f32[512]{0:T(512)S(1)} %add.210), channel_id=1, source_target_pairs={{0,16},{4,20},{8,24},{12,28},{16,0},{20,4},{24,8},{28,12},{1,17},{... | collective-permute-start | bytes 6152 | tf_op jit(solution)/shard_map/ppermute | solution.py:45
  (2 other events, 25.2 us)
Sparse Core Ops, SparseCore 0:
  14.2 29.0 all-gather.5
  62.2 27.3 all-gather.7
  108.2 27.3 all-gather.9
  154.2 27.3 all-gather.11
  202.1 27.3 all-gather.13
